TPU v7x, 32 devices: a whole 2x2x4 slice. The times are simulated.
32 devices in a mesh: grp: 2 (over x), row: 16 (over z, y, core).
Axes of the slice: x: 2, y: 2, z: 4, core: 2. Of those that a mesh axis runs over, the one named last changes fastest.
Arguments:
- field: bfloat16 [256, 1024, 256], P(('grp', 'row')), parts along dimension 0, may hold values from -8 to 8, as said below
- w_qkv: bfloat16 [256, 768], replicated, may hold values from -0.375 to 0.375
- w_attn: bfloat16 [256, 256], replicated, may hold values from -0.375 to 0.375
- w_inner: bfloat16 [256, 512], replicated, may hold values from -0.375 to 0.375
- w_outer: bfloat16 [512, 256], replicated, may hold values from -0.25 to 0.25
- w_skip: bfloat16 [256, 256], replicated, may hold values from -0.375 to 0.375
- w_modes: bfloat16 [512, 2, 256, 256], P('row'), may hold values from -0.25 to 0.25
Outputs:
- result: bfloat16 [256, 1024, 256], P(('grp', 'row')), parts along dimension 0
There are 2 independent parts, one for each index of `grp`. A program takes and returns all parts, laid end to end along the dimension named above; an argument that names none is the same for every part. Nothing has to cross between parts.
Inputs may be any that keep to these rules, and one draw needn't show every extreme that they name: `field`: features of the slab's cells.
All inputs are finite; a program needn't handle non-finite values.
Results may differ from a plain program's by a relative error of at most 0.004.
The roundings to bfloat16 on the way count: a program that leaves them out, or rounds other values in their place, can miss the bound.
Values may be sent and summed in bfloat16 or wider, within the bound.
No kernel may reach another device: no remote copies, remote signals or barrier semaphores. Data moves between devices by JAX's collectives and lax.ppermute only.
A program may use at most 128 MiB of HBM per device.

v0:
```python
import jax
import jax.numpy as jnp
from jax import lax
from jax.sharding import PartitionSpec as P

HEADS = 4
HD = 64
MH = 32
MW = 16
EPSILON = 1e-05
TWO_PI = 6.283185307179586


def head_norm(blocked, heads):
    shaped = blocked.reshape(blocked.shape[0], heads, -1)
    center = shaped - jnp.mean(shaped, axis=-1, keepdims=True)
    spread = jnp.mean(center * center, axis=-1, keepdims=True)
    return (center * lax.rsqrt(spread + EPSILON)).astype(jnp.bfloat16)


def column_table(columns, modes):
    col_index = jnp.arange(columns, dtype=jnp.int32)
    freqs = jnp.arange(modes, dtype=jnp.int32)
    turns = freqs[:, None] * col_index[None, :] % columns
    angle = turns.astype(jnp.float32) * (TWO_PI / columns)
    return (jnp.cos(angle), jnp.sin(angle))


def row_angles(height, modes, rows_global):
    freqs = jnp.arange(modes, dtype=jnp.int32)
    signed = jnp.where(freqs < modes // 2, freqs, freqs - modes + height)
    turns = signed[:, None] * rows_global[None, :] % height
    angle = turns.astype(jnp.float32) * (TWO_PI / height)
    return (jnp.cos(angle), jnp.sin(angle))


def local(field, w_qkv, w_attn, w_inner, w_outer, w_skip, w_modes):
    strip_rows, columns, channels = field.shape
    highest = lax.Precision.HIGHEST
    height = strip_rows * lax.axis_size("row")
    rows_global = lax.axis_index("row") * strip_rows + jnp.arange(strip_rows, dtype=jnp.int32)
    tokens = field.reshape(-1, channels)
    projected = jnp.dot(tokens, w_qkv, preferred_element_type=jnp.float32)
    queries = projected[:, :channels].astype(jnp.bfloat16).reshape(-1, HEADS, HD)
    key_rows = head_norm(projected[:, channels : 2 * channels], HEADS)
    value_rows = head_norm(projected[:, 2 * channels :], HEADS)
    partial_kv = jnp.einsum(
        "thd,the->hde", key_rows, value_rows, preferred_element_type=jnp.float32
    )
    summed_kv = lax.psum(partial_kv, "row")
    scaled_kv = (summed_kv / (height * columns)).astype(jnp.bfloat16)
    attended = jnp.einsum("thd,hde->the", queries, scaled_kv, preferred_element_type=jnp.float32)
    attended = attended.astype(jnp.bfloat16).reshape(-1, channels)
    first = (
        tokens.astype(jnp.float32) + jnp.dot(attended, w_attn, preferred_element_type=jnp.float32)
    ).astype(jnp.bfloat16)
    hidden = jax.nn.gelu(
        jnp.dot(first, w_inner, preferred_element_type=jnp.float32), approximate=False
    ).astype(jnp.bfloat16)
    second = (
        first.astype(jnp.float32) + jnp.dot(hidden, w_outer, preferred_element_type=jnp.float32)
    ).astype(jnp.bfloat16)
    slab_grid = second.reshape(strip_rows, columns, channels)
    col_cos, col_sin = column_table(columns, MW)
    forward_tab = jnp.concatenate([col_cos, -col_sin], axis=0).T.astype(jnp.bfloat16)
    row_spectra = jnp.einsum(
        "rwc,wk->rkc", slab_grid, forward_tab, preferred_element_type=jnp.float32
    )
    spec_re = row_spectra[:, :MW]
    spec_im = row_spectra[:, MW:]
    row_cos, row_sin = row_angles(height, MH, rows_global)
    coeff_re = jnp.einsum("hr,rkc->hkc", row_cos, spec_re, precision=highest) + jnp.einsum(
        "hr,rkc->hkc", row_sin, spec_im, precision=highest
    )
    coeff_im = jnp.einsum("hr,rkc->hkc", row_cos, spec_im, precision=highest) - jnp.einsum(
        "hr,rkc->hkc", row_sin, spec_re, precision=highest
    )
    term_modes = jnp.concatenate([coeff_re, coeff_im], axis=-1).reshape(MH * MW, 2 * channels)
    owned = lax.psum_scatter(term_modes, "row", scatter_dimension=0, tiled=True)
    owned_b = owned.astype(jnp.bfloat16)
    part_re = owned_b[:, :channels]
    part_im = owned_b[:, channels:]
    mode_re = w_modes[:, 0]
    mode_im = w_modes[:, 1]
    mixed_re = jnp.einsum(
        "mc,mco->mo", part_re, mode_re, preferred_element_type=jnp.float32
    ) - jnp.einsum("mc,mco->mo", part_im, mode_im, preferred_element_type=jnp.float32)
    mixed_im = jnp.einsum(
        "mc,mco->mo", part_re, mode_im, preferred_element_type=jnp.float32
    ) + jnp.einsum("mc,mco->mo", part_im, mode_re, preferred_element_type=jnp.float32)
    mixed = jnp.concatenate([mixed_re, mixed_im], axis=-1).astype(jnp.bfloat16)
    segment = lax.all_gather(mixed, "row", axis=0, tiled=True)
    seg_count = segment.shape[0]
    mode_index = jnp.arange(seg_count, dtype=jnp.int32)
    mode_row = mode_index // MW
    mode_col = mode_index % MW
    signed = jnp.where(mode_row < MH // 2, mode_row, mode_row - MH + height)
    turns = signed[:, None] * rows_global[None, :] % height
    angle = turns.astype(jnp.float32) * (TWO_PI / height)
    seg_cos = jnp.cos(angle)[:, :, None]
    seg_sin = jnp.sin(angle)[:, :, None]
    seg_f = segment.astype(jnp.float32)
    seg_re = seg_f[:, None, :channels]
    seg_im = seg_f[:, None, channels:]
    turned = jnp.concatenate(
        [seg_cos * seg_re - seg_sin * seg_im, seg_cos * seg_im + seg_sin * seg_re], axis=-1
    )
    select = (mode_col[:, None] == jnp.arange(MW, dtype=jnp.int32)[None, :]).astype(jnp.float32)
    back_sum = jnp.einsum("mk,mrc->rkc", select, turned, precision=highest)
    weights_kw = jnp.where(jnp.arange(MW, dtype=jnp.int32) == 0, 1.0, 2.0).astype(jnp.float32) / (
        height * columns
    )
    back = (back_sum * weights_kw[None, :, None]).astype(jnp.bfloat16)
    back_stack = jnp.concatenate([back[..., :channels], back[..., channels:]], axis=1)
    inverse_tab = jnp.concatenate([col_cos, -col_sin], axis=0).astype(jnp.bfloat16)
    spectral = jnp.einsum(
        "rkc,kw->rwc", back_stack, inverse_tab, preferred_element_type=jnp.float32
    )
    skipped = jnp.dot(second, w_skip, preferred_element_type=jnp.float32)
    result = jax.nn.gelu(skipped + spectral.reshape(-1, channels), approximate=False)
    return result.astype(jnp.bfloat16).reshape(strip_rows, columns, channels)


def solution(mesh):
    placed = (P(("grp", "row"), None, None), P(), P(), P(), P(), P(), P("row", None, None, None))
    return jax.shard_map(
        local, mesh=mesh, in_specs=placed, out_specs=P(("grp", "row"), None, None), check_vma=False
    )
```

profile of v0, /device:TPU:0, one launch (start us, length us, event | category | flops | bytes accessed | tf_op | source)
XLA Modules:
  0.0 315.8 jit_solution(15945450065870714248)
XLA Ops:
  6.5 0.0 all-reduce.2.cloned.1.call-start
  6.5 1.0 copy-done
  7.5 12.3 %fusion.165 = f32[8192,768]{0,1:T(8,128)} fusion(bf16[8192,256]{1,0:T(8,128)(2,1)} %bitcast.87, bf16[256,768]{1,0:T(8,128)(2,1)S(1)} %copy-done), kind=kOutput, calls=%fused_computation.221 | convolution fusion | flops 3221225472 | bytes 29753344 | tf_op jit(solution)/shard_map/dot_general | solution.py:43
  19.8 6.6 %bitcast_reduce_fusion.1 = (f32[8192,4]{0,1:T(4,128)S(1)}, f32[8192,4]{0,1:T(4,128)S(1)}) fusion(f32[8192,768]{0,1:T(8,128)} %fusion.165), kind=kLoop, calls=%fused_computation.37 | loop fusion | flops 4128768 | bytes 17039360 | tf_op jit(solution)/shard_map/reduce_sum | solution.py:16
  26.4 0.1 broadcast_multiply_fusion
  26.4 7.2 %multiply_reduce_fusion.1 = (f32[8192,4]{0,1:T(4,128)S(1)}, f32[8192,4]{0,1:T(4,128)S(1)}) fusion(f32[8192,768]{0,1:T(8,128)} %fusion.165, f32[8192,4]{0,1:T(4,128)S(1)} %get-tuple-element.22, f32[8192,4]{0,1:T(4,128)S(1)} %get-tuple-element.21), kind=kLoop, calls=%fused_computation.54 | loop fusion | flops 12517376 | bytes 17301504 | tf_op jit(solution)/shard_map/reduce_sum | solution.py:17
  33.6 0.1 add_rsqrt_fusion
  33.7 0.1 add_rsqrt_fusion.1
  33.7 8.0 %fusion.29 = f32[4,64,64]{1,2,0:T(8,128)} fusion(f32[8192,768]{0,1:T(8,128)} %fusion.165, f32[8192,4]{0,1:T(4,128)S(1)} %add_rsqrt_fusion, f32[8192,4]{0,1:T(4,128)S(1)} %get-tuple-element.21, f32[8192,4]{0,1:T(4,128)S(1)} %add_rsqrt_fusion.1, f32[8192,4]{0,1:T(4,128)S(1)} %get-tuple-element.22), kind=kOutput, calls=%fused_computation.58 | convolution fusion | flops 281018368 | bytes 17367040 | tf_op jit(solution)/shard_map/thd,the->hde/dot_general | solution.py:47
  41.7 0.0 all-reduce.2.cloned.1.call-update
  41.7 0.0 reduce-scatter.2.cloned.1.call-start
  41.8 0.9 sine_negate_fusion
  42.7 0.6 compare_select_fusion.1
  43.3 0.6 iota_add_fusion
  43.8 6.0 %slice.91 = bf16[8192,256]{0,1:T(8,128)(2,1)} slice(f32[8192,768]{0,1:T(8,128)} %fusion.165), slice={[0:8192], [0:256]} | slice | bytes 8388608 | tf_op jit(solution)/shard_map/slice | solution.py:44
  49.8 83.0 %all-reduce.2.cloned.1.call-done = f32[4,64,64]{1,2,0:T(8,128)} async-done(((f32[4,64,64]{1,2,0:T(8,128)}), f32[4,64,64]{1,2,0:T(8,128)}) %all-reduce.2.cloned.1.call-update) | async-done | bytes 65552 | tf_op jit(solution)/shard_map/psum | solution.py:50
  132.8 3.6 %convolution_convert_fusion = bf16[4,64,8192]{2,1,0:T(8,128)(2,1)S(1)} fusion(bf16[8192,4,64]{0,2,1:T(8,128)(2,1)} %bitcast.86, f32[4,64,64]{1,2,0:T(8,128)} %all-reduce.2.cloned.1.call-done), kind=kOutput, calls=%fused_computation.22 | convolution fusion | flops 270565376 | bytes 8454144 | tf_op jit(solution)/shard_map/thd,hde->the/dot_general | solution.py:52
  136.5 0.0 copy-start.9
  136.5 0.0 copy-start.10
  136.5 3.3 %fusion.10 = bf16[8192,256]{1,0:T(8,128)(2,1)} fusion(bf16[8192,256]{0,1:T(8,128)(2,1)S(1)} %bitcast.85, bf16[256,256]{1,0:T(8,128)(2,1)S(1)} %copy-done.6, bf16[8192,256]{1,0:T(8,128)(2,1)S(1)} %bitcast.88), kind=kOutput, calls=%fused_computation.23 | convolution fusion | flops 1080033280 | bytes 12713984 | tf_op jit(solution)/shard_map/dot_general | solution.py:55
  139.8 0.0 copy-done.10
  139.9 0.0 copy-start.7
  139.9 0.0 copy-start.8
  139.9 42.3 %fusion.11 = bf16[8192,256]{1,0:T(8,128)(2,1)} fusion(bf16[512,256]{1,0:T(8,128)(2,1)S(1)} %copy-done.9, bf16[8192,256]{1,0:T(8,128)(2,1)} %fusion.10, bf16[256,512]{1,0:T(8,128)(2,1)S(1)} %copy-done.10), kind=kOutput, calls=%fused_computation.25 | convolution fusion | flops 4573888512 | bytes 8912896 | tf_op jit(solution)/shard_map/dot_general | solution.py:61
  182.2 3.0 convolution_bitcast_fusion
  185.2 0.7 fusion.63
  186.0 0.7 fusion.59
  186.7 0.7 convolution_add_fusion.3
  187.5 0.7 convolution_subtract_fusion
  188.2 0.1 pad_maximum_fusion
  188.4 1.6 copy.16
  189.9 0.0 reduce-scatter.2.cloned.1.call-update
  190.0 0.2 fusion.89
  190.2 59.1 %reduce-scatter.2.cloned.1.call-done = f32[32,512]{1,0:T(8,128)} async-done(((f32[512,512]{1,0:T(8,128)}), f32[32,512]{1,0:T(8,128)}) %reduce-scatter.2.cloned.1.call-update) | async-done | bytes 65552 | tf_op jit(solution)/shard_map/reduce_scatter | solution.py:79
  249.3 0.8 convert_element_type.85
  250.1 2.8 fusion.36
  253.0 2.8 fusion.30
  255.8 2.8 fusion.32
  258.6 2.8 fusion.34
  261.5 20.9 %all_gather.3 = bf16[512,512]{1,0:T(8,128)(2,1)S(1)} all-gather(bf16[32,512]{1,0:T(8,128)(2,1)S(1)} %pad_maximum_fusion.1), channel_id=1, replica_groups=mesh['grp'=2,'row'=16] {'row'}, dimensions={0}, use_global_device_ids=true | all-gather | bytes 557056 | tf_op jit(solution)/shard_map/all_gather | solution.py:92
  282.4 0.1 fusion.162
  282.5 1.3 multiply_subtract_fusion
  283.7 0.0 copy-start.3
  283.7 0.0 copy-start.11
  283.8 2.8 fusion.52
  286.6 1.3 fusion.55
  287.9 0.0 copy-start.1
  287.9 21.0 %fusion.14 = bf16[8192,256]{1,0:T(8,128)(2,1)} fusion(f32[8192,256]{1,0:T(8,128)S(1)} %bitcast.89, bf16[8192,256]{1,0:T(8,128)(2,1)S(1)} %copy-done.3, bf16[256,256]{1,0:T(8,128)(2,1)S(1)} %copy-done.11), kind=kOutput, calls=%fused_computation.28 | convolution fusion | flops 1212153856 | bytes 16908288 | tf_op jit(solution)/shard_map/dot_general | solution.py:119
  (24 shorter events, 0.1 us)
Async XLA Ops:
  6.5 1.0 copy-start
  6.5 126.3 %all-reduce.2.cloned.1.call-start = ((), (), s32[]{:S(2)}) async-start(), calls=%async_computation.1 | async-start | bytes 262144 | tf_op jit(solution)/shard_map/psum | solution.py:50
  41.7 207.5 %reduce-scatter.2.cloned.1.call-start = ((), (), s32[]{:S(2)}) async-start(), calls=%async_computation.2 | async-start | bytes 1114112 | tf_op jit(solution)/shard_map/reduce_scatter | solution.py:79
  49.8 86.7 %copy-start.6 = (bf16[256,256]{1,0:T(8,128)(2,1)S(1)}, bf16[256,256]{1,0:T(8,128)(2,1)}, u32[]{:S(2)}) copy-start(bf16[256,256]{1,0:T(8,128)(2,1)} %param.9) | copy-start | bytes 393220
  132.8 3.7 %copy-start.2 = (bf16[8,1024,256]{2,1,0:T(8,128)(2,1)S(1)}, bf16[8,1024,256]{2,1,0:T(8,128)(2,1)}, u32[]{:S(2)}) copy-start(bf16[8,1024,256]{2,1,0:T(8,128)(2,1)} %param.7) | copy-start | bytes 12582916
  136.5 3.4 %copy-start.9 = (bf16[512,256]{1,0:T(8,128)(2,1)S(1)}, bf16[512,256]{1,0:T(8,128)(2,1)}, u32[]{:S(2)}) copy-start(bf16[512,256]{1,0:T(8,128)(2,1)} %param.11) | copy-start | bytes 786436
  136.5 3.4 %copy-start.10 = (bf16[256,512]{1,0:T(8,128)(2,1)S(1)}, bf16[256,512]{1,0:T(8,128)(2,1)}, u32[]{:S(2)}) copy-start(bf16[256,512]{1,0:T(8,128)(2,1)} %param.10) | copy-start | bytes 786436
  139.8 42.3 %copy-start.4 = (bf16[16,1024]{1,0:T(8,128)(2,1)S(1)}, bf16[16,1024]{1,0:T(8,128)(2,1)}, u32[]{:S(2)}) copy-start(bf16[16,1024]{1,0:T(8,128)(2,1)} %get-tuple-element.23) | copy-start | bytes 98308
  139.8 42.3 %copy-start.5 = (bf16[16,1024]{1,0:T(8,128)(2,1)S(1)}, bf16[16,1024]{1,0:T(8,128)(2,1)}, u32[]{:S(2)}) copy-start(bf16[16,1024]{1,0:T(8,128)(2,1)} %get-tuple-element.24) | copy-start | bytes 98308
  139.9 45.4 %copy-start.7 = (s32[8]{0:T(128)S(1)}, s32[8]{0:T(128)}, u32[]{:S(2)}) copy-start(s32[8]{0:T(128)} %iota_add_fusion) | copy-start | bytes 100
  139.9 45.4 %copy-start.8 = (s32[32]{0:T(128)S(1)}, s32[32]{0:T(128)}, u32[]{:S(2)}) copy-start(s32[32]{0:T(128)} %compare_select_fusion.1) | copy-start | bytes 388
  283.7 4.2 %copy-start.3 = (bf16[8192,256]{1,0:T(8,128)(2,1)S(1)}, bf16[8192,256]{1,0:T(8,128)(2,1)}, u32[]{:S(2)}) copy-start(bf16[8192,256]{1,0:T(8,128)(2,1)} %fusion.11) | copy-start | bytes 12582916
  283.7 4.2 %copy-start.11 = (bf16[256,256]{1,0:T(8,128)(2,1)S(1)}, bf16[256,256]{1,0:T(8,128)(2,1)}, u32[]{:S(2)}) copy-start(bf16[256,256]{1,0:T(8,128)(2,1)} %param.12) | copy-start | bytes 393220
  287.9 21.1 %copy-start.1 = (bf16[256,768]{1,0:T(8,128)(2,1)S(1)}, bf16[256,768]{1,0:T(8,128)(2,1)}, u32[]{:S(2)}) copy-start(bf16[256,768]{1,0:T(8,128)(2,1)} %param.8) | copy-start | bytes 1179652
Sparse Core Ops, SparseCore 0:
  41.8 90.9 all-reduce.1
  190.1 59.1 reduce-scatter.1
where the time goes:
time: 316 us
  waiting for transfers between devices  142 us (45%)
  matrix products  112 us (35%)
  blocking collectives  20.9 us (7%)
  other arithmetic  18.4 us (6%)
  between operations  13.7 us (4%)
  local copies, waits for them, and re-layouts  8.7 us (3%)
    psum x1, waiting for transfers between devices, local(): summed_kv = lax.psum(partial_kv, 'row')  83 us
    reduce_scatter x1, waiting for transfers between devices, local(): owned = lax.psum_scatter(term_modes, 'row', scatter_dimension=0, tiled=True)  59.1 us
    dot_general x1, matrix products, local(): jnp.dot(hidden, w_outer, preferred_element_type=jnp.float32)  42.3 us
    dot_general x1, matrix products, local(): skipped = jnp.dot(second, w_skip, preferred_element_type=jnp.float32)  21 us
    all_gather x1, blocking collectives, local(): segment = lax.all_gather(mixed, 'row', axis=0, tiled=True)  20.9 us
    dot_general x1, matrix products, local(): projected = jnp.dot(tokens, w_qkv, preferred_element_type=jnp.float32)  12.3 us
    dot_general x1, matrix products, local(): jnp.einsum('thd,the->hde', key_rows, value_rows, preferred_element_type=j...  7.98 us
    reduce_sum x1, other arithmetic, head_norm(): spread = jnp.mean(center * center, axis=-1, keepdims=True)  7.16 us
  transfers between devices with their start and end apart: 2, of which 2 were waited for; matrix products, arithmetic and copies ran while one was open for 3% of the time, Pallas kernels for 0%

commit v1 on v0

--- a/solution.py
+++ b/solution.py
@@ -47,7 +47,10 @@
     partial_kv = jnp.einsum(
         "thd,the->hde", key_rows, value_rows, preferred_element_type=jnp.float32
     )
-    summed_kv = lax.psum(partial_kv, "row")
+    size, summed_kv = (lax.axis_size("row"), partial_kv)
+    for reach in [1 << k for k in range(size.bit_length() - 1)]:
+        swap = [(i, i ^ reach) for i in range(size)]
+        summed_kv = summed_kv + lax.ppermute(summed_kv, "row", swap)
     scaled_kv = (summed_kv / (height * columns)).astype(jnp.bfloat16)
     attended = jnp.einsum("thd,hde->the", queries, scaled_kv, preferred_element_type=jnp.float32)
     attended = attended.astype(jnp.bfloat16).reshape(-1, channels)

time: 316 us -> 250 us (0.79)
  waiting for transfers between devices: 142 us -> 69.7 us
  starting transfers between devices: 0.04 us -> 7.61 us
    psum x1 -> x0, waiting for transfers between devices: 83 us -> none  [local(): summed_kv = lax.psum(partial_kv, 'row')]
    ppermute x0 -> x4, waiting for transfers between devices: none -> 11.3 us  [local(): summed_kv = summed_kv + lax.ppermute(summed_kv, 'row', swap)]
    ppermute x0 -> x4, starting transfers between devices: none -> 7.6 us  [local(): summed_kv = summed_kv + lax.ppermute(summed_kv, 'row', swap)]
  transfers between devices with their start and end apart: 2 -> 5, of which waited for: 2 -> 4; matrix products, arithmetic and copies ran while one was open for 3% -> 3% of each run, Pallas kernels for 0% -> 0%
where the time goes in v1:
time: 250 us
  matrix products  111 us (44%)
  waiting for transfers between devices  69.7 us (28%)
  blocking collectives  20.8 us (8%)
  other arithmetic  18.3 us (7%)
  between operations  13.7 us (5%)
  local copies, waits for them, and re-layouts  8.7 us (3%)
  starting transfers between devices  7.61 us (3%)
    reduce_scatter x1, waiting for transfers between devices, local(): owned = lax.psum_scatter(term_modes, 'row', scatter_dimension=0, tiled=True)  58.3 us
    dot_general x1, matrix products, local(): jnp.dot(hidden, w_outer, preferred_element_type=jnp.float32)  42.3 us
    dot_general x1, matrix products, local(): skipped = jnp.dot(second, w_skip, preferred_element_type=jnp.float32)  21 us
    all_gather x1, blocking collectives, local(): segment = lax.all_gather(mixed, 'row', axis=0, tiled=True)  20.8 us
    dot_general x1, matrix products, local(): projected = jnp.dot(tokens, w_qkv, preferred_element_type=jnp.float32)  12.3 us
    ppermute x4, waiting for transfers between devices, local(): summed_kv = summed_kv + lax.ppermute(summed_kv, 'row', swap)  11.3 us
    ppermute x4, starting transfers between devices, local(): summed_kv = summed_kv + lax.ppermute(summed_kv, 'row', swap)  7.6 us
    dot_general x1, matrix products, local(): jnp.einsum('thd,the->hde', key_rows, value_rows, preferred_element_type=j...  7.26 us
  transfers between devices with their start and end apart: 5, of which 4 were waited for; matrix products, arithmetic and copies ran while one was open for 3% of the time, Pallas kernels for 0%

profile of v1, /device:TPU:0, one launch (start us, length us, event | category | flops | bytes accessed | tf_op | source)
XLA Modules:
  0.0 250.0 jit_solution(17334357402830248410)
XLA Ops:
  6.5 1.0 copy-done
  7.5 12.3 %fusion.165 = f32[8192,768]{0,1:T(8,128)} fusion(bf16[8192,256]{1,0:T(8,128)(2,1)} %bitcast.87, bf16[256,768]{1,0:T(8,128)(2,1)S(1)} %copy-done), kind=kOutput, calls=%fused_computation.221 | convolution fusion | flops 3221225472 | bytes 29753344 | tf_op jit(solution)/shard_map/dot_general | solution.py:43
  19.8 6.6 %bitcast_reduce_fusion.1 = (f32[8192,4]{0,1:T(4,128)S(1)}, f32[8192,4]{0,1:T(4,128)S(1)}) fusion(f32[8192,768]{0,1:T(8,128)} %fusion.165), kind=kLoop, calls=%fused_computation.37 | loop fusion | flops 4128768 | bytes 17039360 | tf_op jit(solution)/shard_map/reduce_sum | solution.py:16
  26.4 0.1 broadcast_multiply_fusion
  26.4 7.2 %multiply_reduce_fusion.1 = (f32[8192,4]{0,1:T(4,128)S(1)}, f32[8192,4]{0,1:T(4,128)S(1)}) fusion(f32[8192,768]{0,1:T(8,128)} %fusion.165, f32[8192,4]{0,1:T(4,128)S(1)} %get-tuple-element.22, f32[8192,4]{0,1:T(4,128)S(1)} %get-tuple-element.21), kind=kLoop, calls=%fused_computation.54 | loop fusion | flops 12517376 | bytes 17301504 | tf_op jit(solution)/shard_map/reduce_sum | solution.py:17
  33.6 0.1 add_rsqrt_fusion.1
  33.7 0.1 add_rsqrt_fusion
  33.7 7.3 %fusion.29 = f32[4,64,64]{2,1,0:T(8,128)S(1)} fusion(f32[8192,768]{0,1:T(8,128)} %fusion.165, f32[8192,4]{0,1:T(4,128)S(1)} %add_rsqrt_fusion, f32[8192,4]{0,1:T(4,128)S(1)} %get-tuple-element.21, f32[8192,4]{0,1:T(4,128)S(1)} %add_rsqrt_fusion.1, f32[8192,4]{0,1:T(4,128)S(1)} %get-tuple-element.22), kind=kOutput, calls=%fused_computation.58 | convolution fusion | flops 281018368 | bytes 17367040 | tf_op jit(solution)/shard_map/thd,the->hde/dot_general | solution.py:47
  41.0 0.6 collective-permute-start
  41.5 6.0 %slice.91 = bf16[8192,256]{0,1:T(8,128)(2,1)} slice(f32[8192,768]{0,1:T(8,128)} %fusion.165), slice={[0:8192], [0:256]} | slice | bytes 8388608 | tf_op jit(solution)/shard_map/slice | solution.py:44
  47.5 0.0 collective-permute-done
  47.5 2.6 %collective-permute-start.1 = (f32[4,64,64]{2,1,0:T(8,128)S(1)}, f32[4,64,64]{2,1,0:T(8,128)S(1)}, u32[]{:S(2)}, u32[]{:S(2)}) collective-permute-start(f32[4,64,64]{2,1,0:T(8,128)S(1)} %add.130), channel_id=1, source_target_pairs={{0,2},{1,3},{2,0},{3,1},{4,6},{5,7},{6,4},{7,5},{8,10},{9,11},{10,... | collective-permute-start | bytes 196616 | tf_op jit(solution)/shard_map/ppermute | solution.py:53
  50.1 0.9 sine_negate_fusion
  51.0 3.3 %collective-permute-done.1 = f32[4,64,64]{2,1,0:T(8,128)S(1)} collective-permute-done((f32[4,64,64]{2,1,0:T(8,128)S(1)}, f32[4,64,64]{2,1,0:T(8,128)S(1)}, u32[]{:S(2)}, u32[]{:S(2)}) %collective-permute-start.1) | collective-permute-done | bytes 65568 | tf_op jit(solution)/shard_map/ppermute | solution.py:53
  54.3 1.9 collective-permute-start.2
  56.2 0.5 compare_select_fusion.1
  56.7 3.0 %collective-permute-done.2 = f32[4,64,64]{2,1,0:T(8,128)S(1)} collective-permute-done((f32[4,64,64]{2,1,0:T(8,128)S(1)}, f32[4,64,64]{2,1,0:T(8,128)S(1)}, u32[]{:S(2)}, u32[]{:S(2)}) %collective-permute-start.2) | collective-permute-done | bytes 65568 | tf_op jit(solution)/shard_map/ppermute | solution.py:53
  59.7 2.6 %collective-permute-start.3 = (f32[4,64,64]{2,1,0:T(8,128)S(1)}, f32[4,64,64]{2,1,0:T(8,128)S(1)}, u32[]{:S(2)}, u32[]{:S(2)}) collective-permute-start(f32[4,64,64]{2,1,0:T(8,128)S(1)} %add.132), channel_id=1, source_target_pairs={{0,8},{1,9},{2,10},{3,11},{4,12},{5,13},{6,14},{7,15},{8,0},{9,1},... | collective-permute-start | bytes 196616 | tf_op jit(solution)/shard_map/ppermute | solution.py:53
  62.3 0.5 iota_add_fusion
  62.8 5.1 %collective-permute-done.3 = f32[4,64,64]{2,1,0:T(8,128)S(1)} collective-permute-done((f32[4,64,64]{2,1,0:T(8,128)S(1)}, f32[4,64,64]{2,1,0:T(8,128)S(1)}, u32[]{:S(2)}, u32[]{:S(2)}) %collective-permute-start.3) | collective-permute-done | bytes 65568 | tf_op jit(solution)/shard_map/ppermute | solution.py:53
  67.9 3.5 %convolution_convert_fusion = bf16[4,64,8192]{2,1,0:T(8,128)(2,1)S(1)} fusion(bf16[8192,4,64]{0,2,1:T(8,128)(2,1)} %bitcast.86, f32[4,64,64]{2,1,0:T(8,128)S(1)} %add.132, f32[4,64,64]{2,1,0:T(8,128)S(1)} %collective-permute-done.3), kind=kOutput, calls=%fused_computation.22 | convolution fusion | flops 270581760 | bytes 8519680 | tf_op jit(solution)/shard_map/thd,hde->the/dot_general | solution.py:55
  71.4 0.0 copy-start.9
  71.4 0.0 copy-start.10
  71.5 3.3 %fusion.10 = bf16[8192,256]{1,0:T(8,128)(2,1)} fusion(bf16[8192,256]{0,1:T(8,128)(2,1)S(1)} %bitcast.85, bf16[256,256]{1,0:T(8,128)(2,1)S(1)} %copy-done.6, bf16[8192,256]{1,0:T(8,128)(2,1)S(1)} %bitcast.88), kind=kOutput, calls=%fused_computation.23 | convolution fusion | flops 1080033280 | bytes 12713984 | tf_op jit(solution)/shard_map/dot_general | solution.py:58
  74.8 42.3 %fusion.11 = bf16[8192,256]{1,0:T(8,128)(2,1)} fusion(bf16[512,256]{1,0:T(8,128)(2,1)S(1)} %copy-done.9, bf16[8192,256]{1,0:T(8,128)(2,1)} %fusion.10, bf16[256,512]{1,0:T(8,128)(2,1)S(1)} %copy-done.10), kind=kOutput, calls=%fused_computation.25 | convolution fusion | flops 4573888512 | bytes 8912896 | tf_op jit(solution)/shard_map/dot_general | solution.py:64
  117.1 3.0 %convolution_bitcast_fusion = f32[8,32,256]{2,1,0:T(8,128)S(1)} fusion(bf16[8,1024,256]{2,1,0:T(8,128)(2,1)} %bitcast.90, bf16[16,1024]{1,0:T(8,128)(2,1)S(1)} %copy-done.4, bf16[16,1024]{1,0:T(8,128)(2,1)S(1)} %copy-done.5), kind=kOutput, calls=%fused_computation.79 | convolution fusion | flops 134348800 | bytes 4521984 | tf_op jit(solution)/shard_map/rwc,wk->rkc/dot_general | solution.py:69
  120.2 0.7 fusion.63
  120.9 0.7 fusion.59
  121.7 0.7 convolution_add_fusion.3
  122.4 0.7 convolution_subtract_fusion
  123.2 0.1 pad_maximum_fusion
  123.3 1.6 copy.18
  124.9 0.0 reduce-scatter.2.cloned.1.call-update
  124.9 0.2 fusion.89
  125.1 58.3 %reduce-scatter.2.cloned.1.call-done = f32[32,512]{1,0:T(8,128)} async-done(((f32[512,512]{1,0:T(8,128)}), f32[32,512]{1,0:T(8,128)}) %reduce-scatter.2.cloned.1.call-update) | async-done | bytes 65552 | tf_op jit(solution)/shard_map/reduce_scatter | solution.py:82
  183.4 0.8 convert_element_type.85
  184.3 2.8 %fusion.30 = f32[32,1,256]{2,1,0:T(1,128)S(1)} fusion(bf16[32,2,256,256]{3,2,1,0:T(8,128)(2,1)} %param.13, bf16[32,256,1]{1,0,2:T(8,128)(2,1)S(1)} %get-tuple-element.17), kind=kOutput, calls=%fused_computation.59 | convolution fusion | flops 4194304 | bytes 4243456 | tf_op jit(solution)/shard_map/mc,mco->mo/dot_general | solution.py:91
  187.1 2.8 %fusion.36 = f32[32,1,256]{2,1,0:T(1,128)S(1)} fusion(bf16[32,2,256,256]{3,2,1,0:T(8,128)(2,1)} %param.13, bf16[32,256,1]{1,0,2:T(8,128)(2,1)S(1)} %get-tuple-element.17), kind=kOutput, calls=%fused_computation.65 | convolution fusion | flops 4194304 | bytes 4243456 | tf_op jit(solution)/shard_map/mc,mco->mo/dot_general | solution.py:88
  190.0 2.8 %fusion.34 = f32[32,1,256]{2,1,0:T(1,128)S(1)} fusion(bf16[32,2,256,256]{3,2,1,0:T(8,128)(2,1)} %param.13, bf16[32,256,1]{1,0,2:T(8,128)(2,1)S(1)} %get-tuple-element.18), kind=kOutput, calls=%fused_computation.63 | convolution fusion | flops 4194304 | bytes 4243456 | tf_op jit(solution)/shard_map/mc,mco->mo/dot_general | solution.py:93
  192.8 2.8 %fusion.32 = f32[32,1,256]{2,1,0:T(1,128)S(1)} fusion(bf16[32,2,256,256]{3,2,1,0:T(8,128)(2,1)} %param.13, bf16[32,256,1]{1,0,2:T(8,128)(2,1)S(1)} %get-tuple-element.18), kind=kOutput, calls=%fused_computation.61 | convolution fusion | flops 4194304 | bytes 4243456 | tf_op jit(solution)/shard_map/mc,mco->mo/dot_general | solution.py:90
  195.7 20.8 %all_gather.3 = bf16[512,512]{1,0:T(8,128)(2,1)S(1)} all-gather(bf16[32,512]{1,0:T(8,128)(2,1)S(1)} %pad_maximum_fusion.1), channel_id=1, replica_groups=mesh['grp'=2,'row'=16] {'row'}, dimensions={0}, use_global_device_ids=true | all-gather | bytes 557056 | tf_op jit(solution)/shard_map/all_gather | solution.py:95
  216.5 0.1 fusion.162
  216.6 1.3 multiply_subtract_fusion
  217.9 0.0 copy-start.11
  217.9 2.8 %fusion.52 = bf16[8,16,512]{2,1,0:T(8,128)(2,1)S(1)} fusion(f32[512,8,256]{2,0,1:T(8,128)S(1)} %get-tuple-element.10, f32[512,8,256]{2,0,1:T(8,128)S(1)} %get-tuple-element.9, f32[16]{0:T(128)S(1)} %fusion.110, s32[512]{0:T(512)S(1)} %fusion.97), kind=kOutput, calls=%fused_computation.82 | convolution fusion | flops 404889600 | bytes 8521792 | tf_op jit(solution)/shard_map/mk,mrc->rkc/dot_general | solution.py:112
  220.8 1.3 fusion.55
  222.1 0.0 copy-start.1
  222.1 21.0 %fusion.14 = bf16[8192,256]{1,0:T(8,128)(2,1)} fusion(f32[8192,256]{1,0:T(8,128)S(1)} %bitcast.89, bf16[8192,256]{1,0:T(8,128)(2,1)S(1)} %copy-done.3, bf16[256,256]{1,0:T(8,128)(2,1)S(1)} %copy-done.11), kind=kOutput, calls=%fused_computation.28 | convolution fusion | flops 1212153856 | bytes 16908288 | tf_op jit(solution)/shard_map/dot_general | solution.py:122
  (32 shorter events, 0.2 us)
Async XLA Ops:
  6.5 1.0 copy-start
  6.5 176.9 %reduce-scatter.2.cloned.1.call-start = ((), (), s32[]{:S(2)}) async-start(), calls=%async_computation.1 | async-start | bytes 1114112 | tf_op jit(solution)/shard_map/reduce_scatter | solution.py:82
  41.0 6.5 %collective-permute-start = (f32[4,64,64]{2,1,0:T(8,128)S(1)}, f32[4,64,64]{2,1,0:T(8,128)S(1)}, u32[]{:S(2)}, u32[]{:S(2)}) collective-permute-start(f32[4,64,64]{2,1,0:T(8,128)S(1)} %fusion.29), channel_id=1, source_target_pairs={{0,1},{1,0},{2,3},{3,2},{4,5},{5,4},{6,7},{7,6},{8,9},{9,8},{10,11... | collective-permute-start | bytes 196616 | tf_op jit(solution)/shard_map/ppermute | solution.py:53
  47.5 23.9 %copy-start.6 = (bf16[256,256]{1,0:T(8,128)(2,1)S(1)}, bf16[256,256]{1,0:T(8,128)(2,1)}, u32[]{:S(2)}) copy-start(bf16[256,256]{1,0:T(8,128)(2,1)} %param.9) | copy-start | bytes 393220
  47.5 23.9 %copy-start.2 = (bf16[8,1024,256]{2,1,0:T(8,128)(2,1)S(1)}, bf16[8,1024,256]{2,1,0:T(8,128)(2,1)}, u32[]{:S(2)}) copy-start(bf16[8,1024,256]{2,1,0:T(8,128)(2,1)} %param.7) | copy-start | bytes 12582916
  47.5 6.7 %collective-permute-start.1 = (f32[4,64,64]{2,1,0:T(8,128)S(1)}, f32[4,64,64]{2,1,0:T(8,128)S(1)}, u32[]{:S(2)}, u32[]{:S(2)}) collective-permute-start(f32[4,64,64]{2,1,0:T(8,128)S(1)} %add.130), channel_id=1, source_target_pairs={{0,2},{1,3},{2,0},{3,1},{4,6},{5,7},{6,4},{7,5},{8,10},{9,11},{10,... | collective-permute-start | bytes 196616 | tf_op jit(solution)/shard_map/ppermute | solution.py:53
  54.3 5.4 %collective-permute-start.2 = (f32[4,64,64]{2,1,0:T(8,128)S(1)}, f32[4,64,64]{2,1,0:T(8,128)S(1)}, u32[]{:S(2)}, u32[]{:S(2)}) collective-permute-start(f32[4,64,64]{2,1,0:T(8,128)S(1)} %add.131), channel_id=1, source_target_pairs={{0,4},{1,5},{2,6},{3,7},{4,0},{5,1},{6,2},{7,3},{8,12},{9,13},{10,... | collective-permute-start | bytes 196616 | tf_op jit(solution)/shard_map/ppermute | solution.py:53
  59.7 8.2 %collective-permute-start.3 = (f32[4,64,64]{2,1,0:T(8,128)S(1)}, f32[4,64,64]{2,1,0:T(8,128)S(1)}, u32[]{:S(2)}, u32[]{:S(2)}) collective-permute-start(f32[4,64,64]{2,1,0:T(8,128)S(1)} %add.132), channel_id=1, source_target_pairs={{0,8},{1,9},{2,10},{3,11},{4,12},{5,13},{6,14},{7,15},{8,0},{9,1},... | collective-permute-start | bytes 196616 | tf_op jit(solution)/shard_map/ppermute | solution.py:53
  71.4 3.4 %copy-start.9 = (bf16[512,256]{1,0:T(8,128)(2,1)S(1)}, bf16[512,256]{1,0:T(8,128)(2,1)}, u32[]{:S(2)}) copy-start(bf16[512,256]{1,0:T(8,128)(2,1)} %param.11) | copy-start | bytes 786436
  71.4 3.4 %copy-start.10 = (bf16[256,512]{1,0:T(8,128)(2,1)S(1)}, bf16[256,512]{1,0:T(8,128)(2,1)}, u32[]{:S(2)}) copy-start(bf16[256,512]{1,0:T(8,128)(2,1)} %param.10) | copy-start | bytes 786436
  74.8 42.3 %copy-start.4 = (bf16[16,1024]{1,0:T(8,128)(2,1)S(1)}, bf16[16,1024]{1,0:T(8,128)(2,1)}, u32[]{:S(2)}) copy-start(bf16[16,1024]{1,0:T(8,128)(2,1)} %get-tuple-element.23) | copy-start | bytes 98308
  74.8 42.3 %copy-start.5 = (bf16[16,1024]{1,0:T(8,128)(2,1)S(1)}, bf16[16,1024]{1,0:T(8,128)(2,1)}, u32[]{:S(2)}) copy-start(bf16[16,1024]{1,0:T(8,128)(2,1)} %get-tuple-element.24) | copy-start | bytes 98308
  74.8 45.4 %copy-start.7 = (s32[8]{0:T(128)S(1)}, s32[8]{0:T(128)}, u32[]{:S(2)}) copy-start(s32[8]{0:T(128)} %iota_add_fusion) | copy-start | bytes 100
  74.8 45.4 %copy-start.8 = (s32[32]{0:T(128)S(1)}, s32[32]{0:T(128)}, u32[]{:S(2)}) copy-start(s32[32]{0:T(128)} %compare_select_fusion.1) | copy-start | bytes 388
  217.9 4.2 %copy-start.3 = (bf16[8192,256]{1,0:T(8,128)(2,1)S(1)}, bf16[8192,256]{1,0:T(8,128)(2,1)}, u32[]{:S(2)}) copy-start(bf16[8192,256]{1,0:T(8,128)(2,1)} %fusion.11) | copy-start | bytes 12582916
  217.9 4.2 %copy-start.11 = (bf16[256,256]{1,0:T(8,128)(2,1)S(1)}, bf16[256,256]{1,0:T(8,128)(2,1)}, u32[]{:S(2)}) copy-start(bf16[256,256]{1,0:T(8,128)(2,1)} %param.12) | copy-start | bytes 393220
  222.1 21.1 %copy-start.1 = (bf16[256,768]{1,0:T(8,128)(2,1)S(1)}, bf16[256,768]{1,0:T(8,128)(2,1)}, u32[]{:S(2)}) copy-start(bf16[256,768]{1,0:T(8,128)(2,1)} %param.8) | copy-start | bytes 1179652
Sparse Core Ops, SparseCore 0:
  125.0 58.3 reduce-scatter.1
